TPU v7x, 128 devices: a whole 4x4x4 slice. The times are simulated.
128 devices in a mesh: dp: 8 (over z, core), tensor: 16 (over y, x).
Axes of the slice: x: 4, y: 4, z: 4, core: 2. Of those that a mesh axis runs over, the one named last changes fastest.
Arguments:
- residues: bfloat16 [4096, 1024], P('dp'), may hold values from -40 to 40
- block_protein: int32 [32], P('dp'), may hold values from 0 to 31, as said below
- protein_length: int32 [32], replicated, may hold values from 0 to 256, as said below
- decoder_group: int32 [32], replicated, may hold values from 0 to 7, as said below
- enc_gain: float32 [1024], replicated, may hold values from 0.1 to 1.9
- enc_query: bfloat16 [1024, 16384], P(None, 'tensor'), may hold values from -2 to 2
- enc_key: bfloat16 [1024, 16384], P(None, 'tensor'), may hold values from -2 to 2
- enc_value: bfloat16 [1024, 16384], P(None, 'tensor'), may hold values from -0.1875 to 0.1875
- enc_out: bfloat16 [16384, 1024], P('tensor'), may hold values from -0.1875 to 0.1875
- decoder_states: bfloat16 [3072, 1024], P('dp'), may hold values from -40 to 40
- query_protein: int32 [3072], P('dp'), may hold values from 0 to 31, as said below
- dec_gain: float32 [1024], replicated, may hold values from 0.1 to 1.9
- final_gain: float32 [1024], replicated, may hold values from 0.1 to 1.9
- cross_query: bfloat16 [1024, 16384], P(None, 'tensor'), may hold values from -2 to 2
- cross_key: bfloat16 [1024, 16384], P(None, 'tensor'), may hold values from -2 to 2
- cross_value: bfloat16 [1024, 16384], P(None, 'tensor'), may hold values from -0.1875 to 0.1875
- cross_out: bfloat16 [16384, 1024], P('tensor'), may hold values from -0.1875 to 0.1875
Outputs:
- encoded: bfloat16 [4096, 1024], P('dp', 'tensor')
- decoded: bfloat16 [3072, 1024], P(('dp', 'tensor'))
Inputs may be any that keep to these rules, and one draw needn't show every extreme that they name: `block_protein`: block b of dp group d names a protein id from d * 4 to (d + 1) * 4 - 1; the blocks of one protein are consecutive and the ids rise along a group's blocks. `protein_length`: A protein of n blocks has a length from (n - 1) * 128 + 1 to n * 128; an id that no block names has length 0; no protein spans more than 2 blocks. `decoder_group`: at most 2 blocks of one dp group belong to proteins of one decoder group, and in every draw some decoder group gets exactly 2 blocks from every dp group; every decoder group owns a protein of positive length. `query_protein`: query row i names a protein of positive length whose decoder group is i // 384.
All inputs are finite; a program needn't handle non-finite values.
Results may differ from a plain program's by a relative error of at most 0.017.
Values may be sent and summed in bfloat16 or wider, within the bound.
No kernel may reach another device: no remote copies, remote signals or barrier semaphores. Data moves between devices by JAX's collectives and lax.ppermute only.
A program may use at most 128 MiB of HBM per device.

v0:
```python
import jax
import jax.numpy as jnp
from jax import lax
from jax.sharding import PartitionSpec as P

HEAD_DIM = 128
BLOCK = 128
EPSILON = 1e-06
MASKED = -1000000000.0


def split_up(x, dim, size):
    before, after = (x.shape[:dim], x.shape[dim + 1 :])
    return jnp.moveaxis(x.reshape(*before, size, -1, *after), dim, 0)


def sent_and_summed(x, axis, dim):
    blocks = split_up(x, dim, lax.axis_size(axis))
    arrived = lax.all_to_all(blocks, axis, split_axis=0, concat_axis=0, tiled=True)
    return arrived.sum(axis=0)


def summed_on_arrival(x, axis, dim):
    blocks = split_up(x, dim, lax.axis_size(axis))
    arrived = lax.all_to_all(blocks, axis, split_axis=0, concat_axis=0, tiled=True)
    return arrived.astype(jnp.float32).sum(axis=0)


def row_scale(matrix):
    values = matrix.astype(jnp.float32)
    return lax.rsqrt(jnp.mean(values * values, axis=1, keepdims=True) + EPSILON)


def table_lookup(indices, table):
    match = indices[:, None] == jnp.arange(table.shape[0], dtype=jnp.int32)[None, :]
    return jnp.sum(jnp.where(match, table[None, :], 0), axis=1)


def attend(queries, keys, values, allowed):
    count = queries.shape[0]
    heads = queries.shape[1] // HEAD_DIM
    query_heads = queries.reshape(count, heads, HEAD_DIM)
    key_heads = keys.reshape(keys.shape[0], heads, HEAD_DIM)
    value_heads = values.reshape(values.shape[0], heads, HEAD_DIM)
    scores = jnp.einsum(
        "qhd,khd->hqk", query_heads, key_heads, preferred_element_type=jnp.float32
    ) * HEAD_DIM ** (-0.5)
    scores = jnp.where(allowed[None], scores, MASKED)
    top = jnp.max(scores, axis=2, keepdims=True)
    expo = jnp.exp(scores - top)
    total = jnp.sum(expo, axis=2)
    weights = expo.astype(jnp.bfloat16)
    context = jnp.einsum("hqk,khd->qhd", weights, value_heads, preferred_element_type=jnp.float32)
    context = context / jnp.transpose(total)[:, :, None]
    return context.reshape(count, heads * HEAD_DIM).astype(jnp.bfloat16)


def body(
    residues,
    block_protein,
    protein_length,
    decoder_group,
    enc_gain,
    enc_query,
    enc_key,
    enc_value,
    enc_out,
    decoder_states,
    query_protein,
    dec_gain,
    final_gain,
    cross_query,
    cross_key,
    cross_value,
    cross_out,
):
    groups = lax.axis_size("dp")
    tensor_count = lax.axis_size("tensor")
    tensor_index = lax.axis_index("tensor")
    tok_rows = residues.shape[0]
    width = residues.shape[1]
    blocks = block_protein.shape[0]
    slots = blocks // 2
    order = jnp.arange(blocks, dtype=jnp.int32)
    same = block_protein[:, None] == block_protein[None, :]
    offset = jnp.sum(same & (order[None, :] < order[:, None]), axis=1)
    live = jnp.clip(table_lookup(block_protein, protein_length) - offset * BLOCK, 0, BLOCK)
    dest = table_lookup(block_protein, decoder_group)
    position = jnp.arange(BLOCK, dtype=jnp.int32)
    token_protein = jnp.broadcast_to(block_protein[:, None], (blocks, BLOCK)).reshape(tok_rows)
    token_valid = (position[None, :] < live[:, None]).reshape(tok_rows)
    normed = (residues.astype(jnp.float32) * row_scale(residues) * enc_gain[None, :]).astype(
        jnp.bfloat16
    )
    enc_queries = jnp.dot(normed, enc_query, preferred_element_type=jnp.float32).astype(
        jnp.bfloat16
    )
    enc_keys = jnp.dot(normed, enc_key, preferred_element_type=jnp.float32).astype(jnp.bfloat16)
    enc_values = jnp.dot(normed, enc_value, preferred_element_type=jnp.float32).astype(jnp.bfloat16)
    row_block = min(tok_rows, 512)
    block_count = tok_rows // row_block

    def encode_block(item):
        block_queries, block_owner = item
        permit = (block_owner[:, None] == token_protein[None, :]) & token_valid[None, :]
        return attend(block_queries, enc_keys, enc_values, permit)

    context = lax.map(
        encode_block,
        (
            enc_queries.reshape(block_count, row_block, -1),
            token_protein.reshape(block_count, row_block),
        ),
    )
    context = context.reshape(tok_rows, -1)
    partial_value = jnp.dot(context, enc_out, preferred_element_type=jnp.float32)
    slice_width = width // tensor_count
    column_start = tensor_index * slice_width
    same_dest = dest[:, None] == dest[None, :]
    rank = jnp.sum(same_dest & (order[None, :] < order[:, None]), axis=1)
    place = dest * slots + rank
    target = jnp.arange(groups * slots, dtype=jnp.int32)
    chosen = target[:, None] == place[None, :]
    occupied = jnp.any(chosen, axis=1)
    send_ids = jnp.where(
        occupied, jnp.sum(jnp.where(chosen, block_protein[None, :], 0), axis=1), -1
    )
    send_live = jnp.sum(jnp.where(chosen, live[None, :], 0), axis=1)
    send_meta = jnp.stack([send_ids, send_live], axis=-1).reshape(groups, slots, 2)
    shares = sent_and_summed(partial_value, "tensor", 1)
    own_columns = lax.dynamic_slice_in_dim(residues, column_start, slice_width, 1)
    encoded = (own_columns.astype(jnp.float32) + shares).astype(jnp.bfloat16)
    features = encoded.shape[1]
    stacked = encoded.reshape(blocks, BLOCK * features)
    placed = jnp.dot(
        chosen.astype(jnp.bfloat16), stacked, preferred_element_type=jnp.float32
    ).astype(jnp.bfloat16)
    slice_grid = lax.all_to_all(
        placed.reshape(groups, slots, BLOCK, features),
        "dp",
        split_axis=0,
        concat_axis=0,
        tiled=True,
    )
    meta = lax.all_to_all(send_meta, "dp", split_axis=0, concat_axis=0, tiled=True)
    flat = slice_grid.reshape(-1, slice_width)
    inner = cross_key.shape[1]
    values32 = lax.all_gather(flat, "tensor", axis=1, tiled=True).astype(jnp.float32)
    scaled = (values32 * final_gain[None, :]).astype(jnp.bfloat16)
    key_sum = jnp.dot(scaled, cross_key, preferred_element_type=jnp.float32)
    value_sum = jnp.dot(scaled, cross_value, preferred_element_type=jnp.float32)
    squares = jnp.sum(values32 * values32, axis=1, keepdims=True)
    key_sum, value_sum, squares = (key_sum, value_sum, squares)
    key_scale = lax.rsqrt(squares / width + EPSILON)
    grid_shape = (groups, slots, BLOCK, inner)
    key_grid = (key_sum * key_scale).astype(jnp.bfloat16).reshape(grid_shape)
    value_grid = (value_sum * key_scale).astype(jnp.bfloat16).reshape(grid_shape)
    key_ids = meta[:, :, 0]
    key_live = meta[:, :, 1]
    key_valid = position[None, None, :] < key_live[:, :, None]
    query_rows = decoder_states.shape[0]
    dec_normed = (
        decoder_states.astype(jnp.float32) * row_scale(decoder_states) * dec_gain[None, :]
    ).astype(jnp.bfloat16)
    cross_queries = jnp.dot(dec_normed, cross_query, preferred_element_type=jnp.float32).astype(
        jnp.bfloat16
    )
    allowed = (query_protein[:, None, None, None] == key_ids[None, :, :, None]) & key_valid[None]
    slot_total = groups * slots
    inner_width = key_grid.shape[3]
    cross_context = attend(
        cross_queries,
        key_grid.reshape(slot_total * BLOCK, inner_width),
        value_grid.reshape(slot_total * BLOCK, inner_width),
        allowed.reshape(query_rows, slot_total * BLOCK),
    )
    share_rows = query_rows // tensor_count
    mixed = summed_on_arrival(
        jnp.dot(cross_context, cross_out, preferred_element_type=jnp.float32).astype(jnp.bfloat16),
        "tensor",
        0,
    )
    own_rows = lax.dynamic_slice_in_dim(decoder_states, tensor_index * share_rows, share_rows, 0)
    decoded = (own_rows.astype(jnp.float32) + mixed).astype(jnp.bfloat16)
    return (encoded, decoded)


def solution(mesh):
    in_specs = (
        P("dp", None),
        P("dp"),
        P(),
        P(),
        P(),
        P(None, "tensor"),
        P(None, "tensor"),
        P(None, "tensor"),
        P("tensor", None),
        P("dp", None),
        P("dp"),
        P(),
        P(),
        P(None, "tensor"),
        P(None, "tensor"),
        P(None, "tensor"),
        P("tensor", None),
    )
    out_specs = (P("dp", "tensor"), P(("dp", "tensor"), None))
    return jax.shard_map(body, mesh=mesh, in_specs=in_specs, out_specs=out_specs, check_vma=False)
```

profile of v0, /device:TPU:0, one launch (start us, length us, event | category | flops | bytes accessed | tf_op | source)
XLA Modules:
  0.0 220.1 jit_solution(1068523723538875895)
XLA Ops:
  7.2 1.0 convert_reduce_fusion.2
  8.2 0.7 broadcast_bitcast_fusion
  8.9 0.9 select_reduce_fusion.2
  9.8 0.2 convert_reduce_fusion.1
  10.1 1.5 fusion.17
  11.6 4.4 %fusion.31 = bf16[64,8,8,128]{3,2,1,0:T(8,128)(2,1)} fusion(bf16[1024,1024]{1,0:T(8,128)(2,1)} %param.22, bf16[512,1024]{1,0:T(8,128)(2,1)} %param.17, f32[1024]{0:T(1024)} %param.21, f32[512]{0:T(512)S(1)} %add_rsqrt_fusion.2), kind=kOutput, calls=%fused_computation.46 | convolution fusion | flops 1076363264 | bytes 4200448 | tf_op jit(solution)/shard_map/dot_general | solution.py:95
  16.0 2.3 %fusion.32 = bf16[64,8,8,128]{3,2,1,0:T(8,128)(2,1)} fusion(bf16[1024,1024]{1,0:T(8,128)(2,1)S(1)} %copy-done.11, bf16[512,1024]{1,0:T(8,128)(2,1)S(1)} %copy-done.6, f32[1024]{0:T(1024)S(1)} %copy-done.14, f32[512]{0:T(512)S(1)} %add_rsqrt_fusion.2), kind=kOutput, calls=%fused_computation.47 | convolution fusion | flops 1076363264 | bytes 4200448 | tf_op jit(solution)/shard_map/dot_general | solution.py:98
  18.3 2.3 %convolution_convert_fusion.3 = bf16[512,1024]{1,0:T(8,128)(2,1)} fusion(bf16[1024,1024]{1,0:T(8,128)(2,1)S(1)} %copy-done.12, bf16[512,1024]{1,0:T(8,128)(2,1)S(1)} %copy-done.6, f32[1024]{0:T(1024)S(1)} %copy-done.14, f32[512]{0:T(512)S(1)} %add_rsqrt_fusion.2), kind=kOutput, calls=%fused_computation.43 | convolution fusion | flops 1076363264 | bytes 4200448 | tf_op jit(solution)/shard_map/dot_general | solution.py:99
  20.6 2.3 %copy.107 = bf16[512,1024]{0,1:T(8,128)(2,1)} copy(bf16[512,1024]{1,0:T(8,128)(2,1)} %convolution_convert_fusion.3) | data formatting | bytes 2097152 | tf_op jit(solution)/shard_map/while/body/eval_jaxpr/reshape | solution.py:44
  22.9 4.0 %copy.91 = bf16[1024,1024]{0,1:T(8,128)(2,1)} copy(bf16[1024,1024]{1,0:T(8,128)(2,1)} %param.25) | data formatting | bytes 4194304 | tf_op args[8]
  26.9 0.2 compare_and_fusion
  27.1 3.2 %fusion.8 = (f32[8,512]{1,0:T(8,128)S(1)}, f32[8,512,512]{1,2,0:T(8,128)S(1)}) fusion(pred[512,512]{0,1:T(8,128)(4,1)S(1)} %compare_and_fusion, bf16[64,8,8,128]{3,2,1,0:T(8,128)(2,1)} %fusion.32, bf16[64,8,8,128]{3,2,1,0:T(8,128)(2,1)} %fusion.31), kind=kOutput, calls=%fused_computation.16 | convolution fusion | flops 543158272 | bytes 10764288 | tf_op jit(solution)/shard_map/while/body/eval_jaxpr/qhd,khd->hqk/dot_general | solution.py:45
  30.3 1.7 fusion.9
  32.1 2.6 %fusion.20 = bf16[512,8,128]{0,2,1:T(8,128)(2,1)S(1)} fusion(bf16[512,8,128]{0,2,1:T(8,128)(2,1)S(1)} %bitcast.70, f32[8,512,512]{1,2,0:T(8,128)S(1)} %get-tuple-element.33, f32[8,512]{1,0:T(8,128)S(1)} %get-tuple-element.32, pred[512,512]{0,1:T(8,128)(4,1)S(1)} %compare_and_fusion, f32[512,8]{0,1:T(8,128)S(1)} %bitcast.72), kind=kOutput, calls=%fused_computation.31 | convolution fusion | flops 546308096 | bytes 10780672 | tf_op jit(solution)/shard_map/while/body/eval_jaxpr/hqk,khd->qhd/dot_general | solution.py:53
  34.7 2.5 %convolution_bitcast_fusion = f32[16,512,64]{1,2,0:T(8,128)} fusion(bf16[512,1024,1]{0,1,2:T(8,128)(2,1)S(1)} %bitcast.77, bf16[16,64,1024]{2,1,0:T(8,128)(2,1)S(1)} %bitcast.69), kind=kOutput, calls=%fused_computation.34 | convolution fusion | flops 1073741824 | bytes 5242880 | tf_op jit(solution)/shard_map/dot_general | solution.py:116
  37.2 7.2 %all-to-all-start = ((f32[16,512,64]{1,2,0:T(8,128)}), f32[16,512,64]{1,2,0:T(8,128)}, u32[]{:S(2)}, u32[]{:S(2)}) async-start(f32[16,512,64]{1,2,0:T(8,128)} %convolution_bitcast_fusion), calls=%async_computation | async-start | bytes 4194304 | tf_op jit(solution)/shard_map/all_to_all | solution.py:19
  44.5 0.1 constant_dynamic-slice_fusion
  44.6 0.1 copy.111
  44.7 31.5 %all-to-all-done = f32[16,512,64]{1,2,0:T(8,128)} async-done(((f32[16,512,64]{1,2,0:T(8,128)}), f32[16,512,64]{1,2,0:T(8,128)}, u32[]{:S(2)}, u32[]{:S(2)}) %all-to-all-start) | async-done | bytes 2097184 | tf_op jit(solution)/shard_map/all_to_all | solution.py:19
  76.2 1.8 reduce_sum.122
  78.0 0.1 copy.93
  78.2 0.1 reshape.224
  78.3 0.4 convolution_convert_fusion
  78.7 0.5 reshape.225
  79.2 0.2 copy.94
  79.4 12.7 %all_to_all.20 = bf16[8,2,128,64]{2,3,1,0:T(8,128)(2,1)S(1)} all-to-all(bf16[8,2,128,64]{2,3,1,0:T(8,128)(2,1)S(1)} %copy.94), channel_id=1, replica_groups=mesh['dp'=8,'tensor'=16] {'dp'}, dimensions={0} | all-to-all | bytes 524288 | tf_op jit(solution)/shard_map/all_to_all | solution.py:138
  92.1 0.3 copy.95
  92.4 0.9 reshape.226
  93.3 0.1 fusion.45
  93.7 0.6 copy.96
  94.3 3.5 %all-to-all-start.2 = ((s32[8,2,2]{1,2,0:T(2,128)}), s32[8,2,2]{1,2,0:T(2,128)S(1)}, u32[]{:S(2)}, u32[]{:S(2)}) async-start(s32[8,2,2]{1,2,0:T(2,128)} %copy.96), calls=%async_computation.2 | async-start | bytes 16384 | tf_op jit(solution)/shard_map/all_to_all | solution.py:145
  97.8 1.4 fusion.25
  99.2 3.9 %fusion.33 = bf16[48,8,8,128]{3,2,1,0:T(8,128)(2,1)} fusion(bf16[1024,1024]{1,0:T(8,128)(2,1)} %param.30, bf16[384,1024]{1,0:T(8,128)(2,1)} %param.26, f32[1024]{0:T(1024)S(1)} %copy-done.15, f32[384]{0:T(512)S(1)} %add_rsqrt_fusion.1), kind=kOutput, calls=%fused_computation.48 | convolution fusion | flops 807272448 | bytes 3675648 | tf_op jit(solution)/shard_map/dot_general | solution.py:165
  103.3 1.3 bitcast_and_fusion
  104.6 2.2 copy.101
  106.8 33.9 %all-gather.2.cloned.1.call-done = bf16[2048,1024]{0,1:T(8,128)(2,1)} async-done(((bf16[2048,64]{0,1:T(8,128)(2,1)}), bf16[2048,1024]{0,1:T(8,128)(2,1)}) %all-gather.2.cloned.1.call-update) | async-done | bytes 4194320 | tf_op jit(solution)/shard_map/all_gather | solution.py:148
  140.7 3.2 %fusion.7 = f32[2048]{0:T(1024)S(1)} fusion(bf16[2048,1024]{0,1:T(8,128)(2,1)} %all-gather.2.cloned.1.call-done), kind=kLoop, calls=%fused_computation.11 | loop fusion | flops 6289408 | bytes 4202496 | tf_op jit(solution)/shard_map/reduce_sum | solution.py:152
  143.9 0.2 copy-done.2
  144.1 5.6 %multiply_convert_fusion = bf16[2048,1024]{0,1:T(8,128)(2,1)S(1)} fusion(bf16[1024,1024]{1,0:T(8,128)(2,1)S(1)} %copy-done, f32[2048]{0:T(1024)S(1)} %add_rsqrt_fusion, bf16[2048,1024]{0,1:T(8,128)(2,1)S(1)} %copy-done.2, f32[1024]{0:T(1024)S(1)} %copy-done.16), kind=kOutput, calls=%fused_computation.12 | convolution fusion | flops 4305453056 | bytes 10498048 | tf_op jit(solution)/shard_map/dot_general | solution.py:150
  149.8 10.9 %fusion = (f32[8,384]{1,0:T(8,128)S(1)}, f32[8,384,2048]{2,1,0:T(8,128)}) fusion(pred[384,2048]{1,0:T(8,128)(4,1)S(1)} %copy.101, bf16[2048,8,128]{0,2,1:T(8,128)(2,1)S(1)} %bitcast.68, bf16[48,8,8,128]{3,2,1,0:T(8,128)(2,1)S(1)} %copy-done.5), kind=kOutput, calls=%fused_computation.2 | convolution fusion | flops 1629484032 | bytes 30945280 | tf_op jit(solution)/shard_map/qhd,khd->hqk/dot_general | solution.py:45
  160.7 11.7 %fusion.1 = f32[8,384]{1,0:T(8,128)S(1)} fusion(f32[8,384,2048]{2,1,0:T(8,128)} %get-tuple-element.35, f32[8,384]{1,0:T(8,128)S(1)} %get-tuple-element.34, pred[384,2048]{1,0:T(8,128)(4,1)S(1)} %copy.101), kind=kLoop, calls=%fused_computation.3 | loop fusion | flops 25162752 | bytes 25976832 | tf_op jit(solution)/shard_map/reduce_sum | solution.py:51
  172.4 5.6 %multiply_convert_fusion.1 = bf16[2048,1024]{0,1:T(8,128)(2,1)S(1)} fusion(bf16[1024,1024]{1,0:T(8,128)(2,1)S(1)} %copy-done.13, f32[2048]{0:T(1024)S(1)} %add_rsqrt_fusion, bf16[2048,1024]{0,1:T(8,128)(2,1)S(1)} %copy-done.2, f32[1024]{0:T(1024)S(1)} %copy-done.16), kind=kOutput, calls=%fused_computation.13 | convolution fusion | flops 4305453056 | bytes 10498048 | tf_op jit(solution)/shard_map/dot_general | solution.py:151
  178.1 12.2 %fusion.28 = bf16[384,8,128]{0,2,1:T(8,128)(2,1)S(1)} fusion(bf16[2048,8,128]{0,2,1:T(8,128)(2,1)S(1)} %bitcast.76, f32[8,384,2048]{2,1,0:T(8,128)} %get-tuple-element.35, f32[8,384]{1,0:T(8,128)S(1)} %get-tuple-element.34, pred[384,2048]{1,0:T(8,128)(4,1)S(1)} %copy.101, f32[384,8]{0,1:T(8,128)S(1)} %bitcast.75), kind=kOutput, calls=%fused_computation.39 | convolution fusion | flops 1636564992 | bytes 30957568 | tf_op jit(solution)/shard_map/hqk,khd->qhd/dot_general | solution.py:53
  190.3 1.9 convolution_convert_fusion.4
  192.1 5.3 %all-to-all-start.3 = ((bf16[16,24,1024]{2,1,0:T(8,128)(2,1)}), bf16[16,24,1024]{2,1,0:T(8,128)(2,1)S(1)}, u32[]{:S(2)}, u32[]{:S(2)}) async-start(bf16[16,24,1024]{2,1,0:T(8,128)(2,1)} %bitcast.18), calls=%async_computation.3 | async-start | bytes 1572864 | tf_op jit(solution)/shard_map/all_to_all | solution.py:25
  197.4 14.3 %all-to-all-done.3 = bf16[16,24,1024]{2,1,0:T(8,128)(2,1)S(1)} async-done(((bf16[16,24,1024]{2,1,0:T(8,128)(2,1)}), bf16[16,24,1024]{2,1,0:T(8,128)(2,1)S(1)}, u32[]{:S(2)}, u32[]{:S(2)}) %all-to-all-start.3) | async-done | bytes 786464 | tf_op jit(solution)/shard_map/all_to_all | solution.py:25
  211.7 0.1 convert_reduce_fusion
  211.8 1.4 add_convert_fusion.1
  (51 shorter events, 0.7 us)
Async XLA Ops:
  7.2 136.7 %copy-start = (bf16[1024,1024]{1,0:T(8,128)(2,1)S(1)}, bf16[1024,1024]{1,0:T(8,128)(2,1)}, u32[]{:S(2)}) copy-start(bf16[1024,1024]{1,0:T(8,128)(2,1)} %param.31) | copy-start | bytes 6291460
  11.6 4.4 %copy-start.6 = (bf16[512,1024]{1,0:T(8,128)(2,1)S(1)}, bf16[512,1024]{1,0:T(8,128)(2,1)}, u32[]{:S(2)}) copy-start(bf16[512,1024]{1,0:T(8,128)(2,1)} %param.17) | copy-start | bytes 3145732
  11.6 4.4 %copy-start.11 = (bf16[1024,1024]{1,0:T(8,128)(2,1)S(1)}, bf16[1024,1024]{1,0:T(8,128)(2,1)}, u32[]{:S(2)}) copy-start(bf16[1024,1024]{1,0:T(8,128)(2,1)} %param.23) | copy-start | bytes 6291460
  11.6 4.4 %copy-start.14 = (f32[1024]{0:T(1024)S(1)}, f32[1024]{0:T(1024)}, u32[]{:S(2)}) copy-start(f32[1024]{0:T(1024)} %param.21) | copy-start | bytes 12292
  16.0 2.3 %copy-start.12 = (bf16[1024,1024]{1,0:T(8,128)(2,1)S(1)}, bf16[1024,1024]{1,0:T(8,128)(2,1)}, u32[]{:S(2)}) copy-start(bf16[1024,1024]{1,0:T(8,128)(2,1)} %param.24) | copy-start | bytes 6291460
  30.3 1.8 copy-start.7
  32.1 2.6 %copy-start.4 = (bf16[1024,1024]{0,1:T(8,128)(2,1)S(1)}, bf16[1024,1024]{0,1:T(8,128)(2,1)}, u32[]{:S(2)}) copy-start(bf16[1024,1024]{0,1:T(8,128)(2,1)} %copy.91) | copy-start | bytes 6291460
  37.2 39.0 %all-to-all-start = ((f32[16,512,64]{1,2,0:T(8,128)}), f32[16,512,64]{1,2,0:T(8,128)}, u32[]{:S(2)}, u32[]{:S(2)}) async-start(f32[16,512,64]{1,2,0:T(8,128)} %convolution_bitcast_fusion), calls=%async_computation | async-start | bytes 4194304 | tf_op jit(solution)/shard_map/all_to_all | solution.py:19
  44.4 49.0 %copy-start.9 = (s32[4]{0:T(128)S(1)}, s32[4]{0:T(128)}, u32[]{:S(2)}) copy-start(s32[4]{0:T(128)} %param.18) | copy-start | bytes 52
  44.4 54.8 %copy-start.15 = (f32[1024]{0:T(1024)S(1)}, f32[1024]{0:T(1024)}, u32[]{:S(2)}) copy-start(f32[1024]{0:T(1024)} %param.28) | copy-start | bytes 12292
  44.4 96.2 %all-gather.2.cloned.1.call-start = ((), (), s32[]{:S(2)}) async-start(), calls=%async_computation.4 | async-start | bytes 4456448 | tf_op jit(solution)/shard_map/all_gather | solution.py:148
  78.0 25.0 %copy-start.8 = (bf16[512,64]{0,1:T(8,128)(2,1)}, bf16[512,64]{0,1:T(8,128)(2,1)S(1)}, u32[]{:S(2)}) copy-start(bf16[512,64]{0,1:T(8,128)(2,1)S(1)} %add_convert_fusion) | copy-start | bytes 196612
  92.4 10.8 %copy-start.10 = (s32[384]{0:T(512)S(1)}, s32[384]{0:T(512)}, u32[]{:S(2)}) copy-start(s32[384]{0:T(512)} %param.27) | copy-start | bytes 4612
  94.3 8.8 %all-to-all-start.2 = ((s32[8,2,2]{1,2,0:T(2,128)}), s32[8,2,2]{1,2,0:T(2,128)S(1)}, u32[]{:S(2)}, u32[]{:S(2)}) async-start(s32[8,2,2]{1,2,0:T(2,128)} %copy.96), calls=%async_computation.2 | async-start | bytes 16384 | tf_op jit(solution)/shard_map/all_to_all | solution.py:145
  103.1 40.9 %copy-start.16 = (f32[1024]{0:T(1024)S(1)}, f32[1024]{0:T(1024)}, u32[]{:S(2)}) copy-start(f32[1024]{0:T(1024)} %param.29) | copy-start | bytes 12292
  140.7 3.4 %copy-start.2 = (bf16[2048,1024]{0,1:T(8,128)(2,1)S(1)}, bf16[2048,1024]{0,1:T(8,128)(2,1)}, u32[]{:S(2)}) copy-start(bf16[2048,1024]{0,1:T(8,128)(2,1)} %all-gather.2.cloned.1.call-done) | copy-start | bytes 12582916
  144.1 5.6 %copy-start.5 = (bf16[48,8,8,128]{3,2,1,0:T(8,128)(2,1)S(1)}, bf16[48,8,8,128]{3,2,1,0:T(8,128)(2,1)}, u32[]{:S(2)}) copy-start(bf16[48,8,8,128]{3,2,1,0:T(8,128)(2,1)} %fusion.33) | copy-start | bytes 2359300
  160.7 11.7 %copy-start.13 = (bf16[1024,1024]{1,0:T(8,128)(2,1)S(1)}, bf16[1024,1024]{1,0:T(8,128)(2,1)}, u32[]{:S(2)}) copy-start(bf16[1024,1024]{1,0:T(8,128)(2,1)} %param.32) | copy-start | bytes 6291460
  178.0 12.2 %copy-start.3 = (bf16[1024,1024]{1,0:T(8,128)(2,1)S(1)}, bf16[1024,1024]{1,0:T(8,128)(2,1)}, u32[]{:S(2)}) copy-start(bf16[1024,1024]{1,0:T(8,128)(2,1)} %param.33) | copy-start | bytes 6291460
  178.1 35.2 %copy-start.1 = (bf16[1024,1024]{1,0:T(8,128)(2,1)S(1)}, bf16[1024,1024]{1,0:T(8,128)(2,1)}, u32[]{:S(2)}) copy-start(bf16[1024,1024]{1,0:T(8,128)(2,1)} %param.31) | copy-start | bytes 6291460
  192.1 19.6 %all-to-all-start.3 = ((bf16[16,24,1024]{2,1,0:T(8,128)(2,1)}), bf16[16,24,1024]{2,1,0:T(8,128)(2,1)S(1)}, u32[]{:S(2)}, u32[]{:S(2)}) async-start(bf16[16,24,1024]{2,1,0:T(8,128)(2,1)} %bitcast.18), calls=%async_computation.3 | async-start | bytes 1572864 | tf_op jit(solution)/shard_map/all_to_all | solution.py:25
Sparse Core Ops, SparseCore 0:
  93.4 47.2 all-gather.1
where the time goes:
time: 221 us; the launch traced here: 220 us
  waiting for transfers between devices  79.8 us (36%)
  matrix products  57.7 us (26%)
  other arithmetic  27 us (12%)
  starting transfers between devices  16 us (7%)
  between operations  14.4 us (7%)
  blocking collectives  12.7 us (6%)
  local copies, waits for them, and re-layouts  12.6 us (6%)
    all_gather x1, waiting for transfers between devices, body(): lax.all_gather(flat, 'tensor', axis=1, tiled=True).astype(jnp.float32)  33.9 us
    all_to_all x1, waiting for transfers between devices, sent_and_summed(): lax.all_to_all(blocks, axis, split_axis=0, concat_axis=0, tiled=True)  31.5 us
    dot_general x2, matrix products, attend(): jnp.einsum('hqk,khd->qhd', weights, value_heads, preferred_element_type=j...  14.7 us
    all_to_all x1, waiting for transfers between devices, summed_on_arrival(): lax.all_to_all(blocks, axis, split_axis=0, concat_axis=0, tiled=True)  14.3 us
    dot_general x2, matrix products, attend(): jnp.einsum('qhd,khd->hqk', query_heads, key_heads, preferred_element_type...  14.1 us
    reduce_sum x2, other arithmetic, attend(): total = jnp.sum(expo, axis=2)  13.4 us
    all_to_all x1, blocking collectives, body(): lax.all_to_all(placed.reshape(groups, slots, BLOCK, features), 'dp', spli...  12.7 us
    all_to_all x1, starting transfers between devices, sent_and_summed(): lax.all_to_all(blocks, axis, split_axis=0, concat_axis=0, tiled=True)  7.19 us
  transfers between devices with their start and end apart: 4, of which 3 were waited for; matrix products, arithmetic and copies ran while one was open for 5% of the time, Pallas kernels for 0%

commit v1 on v0

--- a/solution.py
+++ b/solution.py
@@ -145,7 +145,7 @@
     meta = lax.all_to_all(send_meta, "dp", split_axis=0, concat_axis=0, tiled=True)
     flat = slice_grid.reshape(-1, slice_width)
     inner = cross_key.shape[1]
-    values32 = lax.all_gather(flat, "tensor", axis=1, tiled=True).astype(jnp.float32)
+    values32 = jnp.concatenate(lax.all_gather(flat, "tensor"), axis=1).astype(jnp.float32)
     scaled = (values32 * final_gain[None, :]).astype(jnp.bfloat16)
     key_sum = jnp.dot(scaled, cross_key, preferred_element_type=jnp.float32)
     value_sum = jnp.dot(scaled, cross_value, preferred_element_type=jnp.float32)

time: 221 us -> 220 us (level)
  no operation moved by 1% of the time
where the time goes in v1:
time: 220 us
  waiting for transfers between devices  79.8 us (36%)
  matrix products  56.5 us (26%)
  other arithmetic  27.6 us (13%)
  starting transfers between devices  16 us (7%)
  between operations  14.4 us (7%)
  local copies, waits for them, and re-layouts  12.7 us (6%)
  blocking collectives  12.7 us (6%)
    all_gather x1, waiting for transfers between devices, body(): lax.all_gather(flat, 'tensor')  33.9 us
    all_to_all x1, waiting for transfers between devices, sent_and_summed(): lax.all_to_all(blocks, axis, split_axis=0, concat_axis=0, tiled=True)  31.5 us
    dot_general x2, matrix products, attend(): jnp.einsum('hqk,khd->qhd', weights, value_heads, preferred_element_type=j...  14.6 us
    all_to_all x1, waiting for transfers between devices, summed_on_arrival(): lax.all_to_all(blocks, axis, split_axis=0, concat_axis=0, tiled=True)  14.3 us
    dot_general x2, matrix products, attend(): jnp.einsum('qhd,khd->hqk', query_heads, key_heads, preferred_element_type...  14.1 us
    reduce_sum x2, other arithmetic, attend(): total = jnp.sum(expo, axis=2)  13.3 us
    all_to_all x1, blocking collectives, body(): lax.all_to_all(placed.reshape(groups, slots, BLOCK, features), 'dp', spli...  12.7 us
    all_to_all x1, starting transfers between devices, sent_and_summed(): lax.all_to_all(blocks, axis, split_axis=0, concat_axis=0, tiled=True)  7.19 us
  transfers between devices with their start and end apart: 4, of which 3 were waited for; matrix products, arithmetic and copies ran while one was open for 5% of the time, Pallas kernels for 0%

profile of v1, /device:TPU:0, one launch (start us, length us, event | category | flops | bytes accessed | tf_op | source)
XLA Modules:
  0.0 219.6 jit_solution(4871414322046743705)
XLA Ops:
  7.2 1.0 convert_reduce_fusion.2
  8.2 0.7 broadcast_bitcast_fusion
  8.9 0.9 select_reduce_fusion.2
  9.8 0.2 convert_reduce_fusion.1
  10.1 1.5 fusion.16
  11.6 4.4 %fusion.28 = bf16[64,8,8,128]{3,2,1,0:T(8,128)(2,1)} fusion(bf16[1024,1024]{1,0:T(8,128)(2,1)} %param.22, bf16[512,1024]{1,0:T(8,128)(2,1)} %param.17, f32[1024]{0:T(1024)} %param.21, f32[512]{0:T(512)S(1)} %add_rsqrt_fusion.2), kind=kOutput, calls=%fused_computation.45 | convolution fusion | flops 1076363264 | bytes 4200448 | tf_op jit(solution)/shard_map/dot_general | solution.py:95
  16.0 2.3 %fusion.29 = bf16[64,8,8,128]{3,2,1,0:T(8,128)(2,1)} fusion(bf16[1024,1024]{1,0:T(8,128)(2,1)S(1)} %copy-done.12, bf16[512,1024]{1,0:T(8,128)(2,1)S(1)} %copy-done.6, f32[1024]{0:T(1024)S(1)} %copy-done.15, f32[512]{0:T(512)S(1)} %add_rsqrt_fusion.2), kind=kOutput, calls=%fused_computation.46 | convolution fusion | flops 1076363264 | bytes 4200448 | tf_op jit(solution)/shard_map/dot_general | solution.py:98
  18.3 2.3 %convolution_convert_fusion.3 = bf16[512,1024]{1,0:T(8,128)(2,1)} fusion(bf16[1024,1024]{1,0:T(8,128)(2,1)S(1)} %copy-done.13, bf16[512,1024]{1,0:T(8,128)(2,1)S(1)} %copy-done.6, f32[1024]{0:T(1024)S(1)} %copy-done.15, f32[512]{0:T(512)S(1)} %add_rsqrt_fusion.2), kind=kOutput, calls=%fused_computation.42 | convolution fusion | flops 1076363264 | bytes 4200448 | tf_op jit(solution)/shard_map/dot_general | solution.py:99
  20.6 2.3 %copy.108 = bf16[512,1024]{0,1:T(8,128)(2,1)} copy(bf16[512,1024]{1,0:T(8,128)(2,1)} %convolution_convert_fusion.3) | data formatting | bytes 2097152 | tf_op jit(solution)/shard_map/while/body/eval_jaxpr/reshape | solution.py:44
  22.9 4.0 %copy.92 = bf16[1024,1024]{0,1:T(8,128)(2,1)} copy(bf16[1024,1024]{1,0:T(8,128)(2,1)} %param.25) | data formatting | bytes 4194304 | tf_op args[8]
  26.9 0.2 compare_and_fusion
  27.1 3.2 %fusion.7 = (f32[8,512]{1,0:T(8,128)S(1)}, f32[8,512,512]{1,2,0:T(8,128)S(1)}) fusion(pred[512,512]{0,1:T(8,128)(4,1)S(1)} %compare_and_fusion, bf16[64,8,8,128]{3,2,1,0:T(8,128)(2,1)} %fusion.29, bf16[64,8,8,128]{3,2,1,0:T(8,128)(2,1)} %fusion.28), kind=kOutput, calls=%fused_computation.15 | convolution fusion | flops 543158272 | bytes 10764288 | tf_op jit(solution)/shard_map/while/body/eval_jaxpr/qhd,khd->hqk/dot_general | solution.py:45
  30.3 1.7 fusion.8
  32.1 2.6 %fusion.19 = bf16[512,8,128]{0,2,1:T(8,128)(2,1)S(1)} fusion(bf16[512,8,128]{0,2,1:T(8,128)(2,1)S(1)} %bitcast.78, f32[8,512,512]{1,2,0:T(8,128)S(1)} %get-tuple-element.33, f32[8,512]{1,0:T(8,128)S(1)} %get-tuple-element.32, pred[512,512]{0,1:T(8,128)(4,1)S(1)} %compare_and_fusion, f32[512,8]{0,1:T(8,128)S(1)} %bitcast.80), kind=kOutput, calls=%fused_computation.30 | convolution fusion | flops 546308096 | bytes 10780672 | tf_op jit(solution)/shard_map/while/body/eval_jaxpr/hqk,khd->qhd/dot_general | solution.py:53
  34.7 2.5 %convolution_bitcast_fusion = f32[16,512,64]{1,2,0:T(8,128)} fusion(bf16[512,1024,1]{0,1,2:T(8,128)(2,1)S(1)} %bitcast.85, bf16[16,64,1024]{2,1,0:T(8,128)(2,1)S(1)} %bitcast.77), kind=kOutput, calls=%fused_computation.33 | convolution fusion | flops 1073741824 | bytes 5242880 | tf_op jit(solution)/shard_map/dot_general | solution.py:116
  37.2 7.2 %all-to-all-start = ((f32[16,512,64]{1,2,0:T(8,128)}), f32[16,512,64]{1,2,0:T(8,128)}, u32[]{:S(2)}, u32[]{:S(2)}) async-start(f32[16,512,64]{1,2,0:T(8,128)} %convolution_bitcast_fusion), calls=%async_computation | async-start | bytes 4194304 | tf_op jit(solution)/shard_map/all_to_all | solution.py:19
  44.5 0.1 constant_dynamic-slice_fusion
  44.6 0.1 copy.112
  44.7 31.5 %all-to-all-done = f32[16,512,64]{1,2,0:T(8,128)} async-done(((f32[16,512,64]{1,2,0:T(8,128)}), f32[16,512,64]{1,2,0:T(8,128)}, u32[]{:S(2)}, u32[]{:S(2)}) %all-to-all-start) | async-done | bytes 2097184 | tf_op jit(solution)/shard_map/all_to_all | solution.py:19
  76.2 1.8 reduce_sum.122
  78.0 0.1 copy.94
  78.2 0.1 reshape.225
  78.3 0.4 convolution_convert_fusion
  78.7 0.5 reshape.226
  79.2 0.2 copy.95
  79.4 12.7 %all_to_all.20 = bf16[8,2,128,64]{2,3,1,0:T(8,128)(2,1)S(1)} all-to-all(bf16[8,2,128,64]{2,3,1,0:T(8,128)(2,1)S(1)} %copy.95), channel_id=1, replica_groups=mesh['dp'=8,'tensor'=16] {'dp'}, dimensions={0} | all-to-all | bytes 524288 | tf_op jit(solution)/shard_map/all_to_all | solution.py:138
  92.1 0.3 copy.96
  92.4 0.9 all_gather_reshape.3
  93.7 0.6 copy.97
  94.3 3.5 %all-to-all-start.2 = ((s32[8,2,2]{1,2,0:T(2,128)}), s32[8,2,2]{1,2,0:T(2,128)S(1)}, u32[]{:S(2)}, u32[]{:S(2)}) async-start(s32[8,2,2]{1,2,0:T(2,128)} %copy.97), calls=%async_computation.2 | async-start | bytes 16384 | tf_op jit(solution)/shard_map/all_to_all | solution.py:145
  97.8 1.4 fusion.22
  99.2 3.9 %fusion.30 = bf16[48,8,8,128]{3,2,1,0:T(8,128)(2,1)} fusion(bf16[1024,1024]{1,0:T(8,128)(2,1)} %param.30, bf16[384,1024]{1,0:T(8,128)(2,1)} %param.26, f32[1024]{0:T(1024)S(1)} %copy-done.16, f32[384]{0:T(512)S(1)} %add_rsqrt_fusion.1), kind=kOutput, calls=%fused_computation.47 | convolution fusion | flops 807272448 | bytes 3675648 | tf_op jit(solution)/shard_map/dot_general | solution.py:165
  103.3 1.3 bitcast_and_fusion
  104.6 2.2 copy.102
  106.8 33.9 %all-gather.2.cloned.1.call-done = bf16[16,2048,64]{1,2,0:T(8,128)(2,1)} async-done(((bf16[1,2048,64]{1,2,0:T(8,128)(2,1)}), bf16[16,2048,64]{1,2,0:T(8,128)(2,1)}) %all-gather.2.cloned.1.call-update) | async-done | bytes 4194320 | tf_op jit(solution)/shard_map/all_gather | solution.py:148
  140.7 3.2 %multiply_reduce_fusion = f32[2048]{0:T(1024)S(1)} fusion(bf16[16,2048,64]{1,2,0:T(8,128)(2,1)} %all-gather.2.cloned.1.call-done), kind=kLoop, calls=%fused_computation.12 | loop fusion | flops 6289408 | bytes 4202496 | tf_op jit(solution)/shard_map/reduce_sum | solution.py:152
  143.9 0.2 copy-done.2
  144.1 0.7 fusion.6
  144.9 5.1 %multiply_convert_fusion = bf16[2048,1024]{0,1:T(8,128)(2,1)S(1)} fusion(bf16[2048,1024]{0,1:T(8,128)(2,1)S(1)} %fusion.6, bf16[1024,1024]{1,0:T(8,128)(2,1)S(1)} %copy-done, f32[2048]{0:T(1024)S(1)} %add_rsqrt_fusion), kind=kOutput, calls=%fused_computation.10 | convolution fusion | flops 4299161600 | bytes 10493952 | tf_op jit(solution)/shard_map/dot_general | solution.py:150
  150.0 5.1 %multiply_convert_fusion.1 = bf16[2048,1024]{0,1:T(8,128)(2,1)S(1)} fusion(bf16[2048,1024]{0,1:T(8,128)(2,1)S(1)} %fusion.6, bf16[1024,1024]{1,0:T(8,128)(2,1)S(1)} %copy-done.14, f32[2048]{0:T(1024)S(1)} %add_rsqrt_fusion), kind=kOutput, calls=%fused_computation.11 | convolution fusion | flops 4299161600 | bytes 10493952 | tf_op jit(solution)/shard_map/dot_general | solution.py:151
  155.1 10.9 %fusion = (f32[8,384]{1,0:T(8,128)S(1)}, f32[8,384,2048]{2,1,0:T(8,128)}) fusion(pred[384,2048]{1,0:T(8,128)(4,1)S(1)} %copy.102, bf16[2048,8,128]{0,2,1:T(8,128)(2,1)S(1)} %bitcast.76, bf16[48,8,8,128]{3,2,1,0:T(8,128)(2,1)S(1)} %copy-done.5), kind=kOutput, calls=%fused_computation.2 | convolution fusion | flops 1629484032 | bytes 30945280 | tf_op jit(solution)/shard_map/qhd,khd->hqk/dot_general | solution.py:45
  166.0 11.6 %fusion.1 = f32[8,384]{1,0:T(8,128)S(1)} fusion(f32[8,384,2048]{2,1,0:T(8,128)} %get-tuple-element.35, f32[8,384]{1,0:T(8,128)S(1)} %get-tuple-element.34, pred[384,2048]{1,0:T(8,128)(4,1)S(1)} %copy.102), kind=kLoop, calls=%fused_computation.3 | loop fusion | flops 25162752 | bytes 25976832 | tf_op jit(solution)/shard_map/reduce_sum | solution.py:51
  177.6 12.0 %fusion.25 = bf16[384,8,128]{0,2,1:T(8,128)(2,1)S(1)} fusion(bf16[2048,8,128]{0,2,1:T(8,128)(2,1)S(1)} %bitcast.84, f32[8,384,2048]{2,1,0:T(8,128)} %get-tuple-element.35, f32[8,384]{1,0:T(8,128)S(1)} %get-tuple-element.34, pred[384,2048]{1,0:T(8,128)(4,1)S(1)} %copy.102, f32[384,8]{0,1:T(8,128)S(1)} %bitcast.83), kind=kOutput, calls=%fused_computation.38 | convolution fusion | flops 1636564992 | bytes 30957568 | tf_op jit(solution)/shard_map/hqk,khd->qhd/dot_general | solution.py:53
  189.7 1.9 convolution_convert_fusion.4
  191.5 5.3 %all-to-all-start.3 = ((bf16[16,24,1024]{2,1,0:T(8,128)(2,1)}), bf16[16,24,1024]{2,1,0:T(8,128)(2,1)S(1)}, u32[]{:S(2)}, u32[]{:S(2)}) async-start(bf16[16,24,1024]{2,1,0:T(8,128)(2,1)} %bitcast.20), calls=%async_computation.3 | async-start | bytes 1572864 | tf_op jit(solution)/shard_map/all_to_all | solution.py:25
  196.8 14.3 %all-to-all-done.3 = bf16[16,24,1024]{2,1,0:T(8,128)(2,1)S(1)} async-done(((bf16[16,24,1024]{2,1,0:T(8,128)(2,1)}), bf16[16,24,1024]{2,1,0:T(8,128)(2,1)S(1)}, u32[]{:S(2)}, u32[]{:S(2)}) %all-to-all-start.3) | async-done | bytes 786464 | tf_op jit(solution)/shard_map/all_to_all | solution.py:25
  211.1 0.1 convert_reduce_fusion
  211.3 1.4 add_convert_fusion.1
  (52 shorter events, 0.8 us)
Async XLA Ops:
  7.2 137.7 %copy-start = (bf16[1024,1024]{1,0:T(8,128)(2,1)S(1)}, bf16[1024,1024]{1,0:T(8,128)(2,1)}, u32[]{:S(2)}) copy-start(bf16[1024,1024]{1,0:T(8,128)(2,1)} %param.31) | copy-start | bytes 6291460
  11.6 4.4 %copy-start.6 = (bf16[512,1024]{1,0:T(8,128)(2,1)S(1)}, bf16[512,1024]{1,0:T(8,128)(2,1)}, u32[]{:S(2)}) copy-start(bf16[512,1024]{1,0:T(8,128)(2,1)} %param.17) | copy-start | bytes 3145732
  11.6 4.4 %copy-start.12 = (bf16[1024,1024]{1,0:T(8,128)(2,1)S(1)}, bf16[1024,1024]{1,0:T(8,128)(2,1)}, u32[]{:S(2)}) copy-start(bf16[1024,1024]{1,0:T(8,128)(2,1)} %param.23) | copy-start | bytes 6291460
  11.6 4.4 %copy-start.15 = (f32[1024]{0:T(1024)S(1)}, f32[1024]{0:T(1024)}, u32[]{:S(2)}) copy-start(f32[1024]{0:T(1024)} %param.21) | copy-start | bytes 12292
  16.0 2.3 %copy-start.13 = (bf16[1024,1024]{1,0:T(8,128)(2,1)S(1)}, bf16[1024,1024]{1,0:T(8,128)(2,1)}, u32[]{:S(2)}) copy-start(bf16[1024,1024]{1,0:T(8,128)(2,1)} %param.24) | copy-start | bytes 6291460
  30.3 1.8 copy-start.7
  32.1 2.6 %copy-start.4 = (bf16[1024,1024]{0,1:T(8,128)(2,1)S(1)}, bf16[1024,1024]{0,1:T(8,128)(2,1)}, u32[]{:S(2)}) copy-start(bf16[1024,1024]{0,1:T(8,128)(2,1)} %copy.92) | copy-start | bytes 6291460
  37.2 39.0 %all-to-all-start = ((f32[16,512,64]{1,2,0:T(8,128)}), f32[16,512,64]{1,2,0:T(8,128)}, u32[]{:S(2)}, u32[]{:S(2)}) async-start(f32[16,512,64]{1,2,0:T(8,128)} %convolution_bitcast_fusion), calls=%async_computation | async-start | bytes 4194304 | tf_op jit(solution)/shard_map/all_to_all | solution.py:19
  44.4 49.0 %copy-start.9 = (s32[4]{0:T(128)S(1)}, s32[4]{0:T(128)}, u32[]{:S(2)}) copy-start(s32[4]{0:T(128)} %param.18) | copy-start | bytes 52
  44.4 54.8 %copy-start.16 = (f32[1024]{0:T(1024)S(1)}, f32[1024]{0:T(1024)}, u32[]{:S(2)}) copy-start(f32[1024]{0:T(1024)} %param.28) | copy-start | bytes 12292
  44.4 96.2 %all-gather.2.cloned.1.call-start = ((), (), s32[]{:S(2)}) async-start(), calls=%async_computation.4 | async-start | bytes 4456448 | tf_op jit(solution)/shard_map/all_gather | solution.py:148
  78.0 25.0 %copy-start.8 = (bf16[512,64]{0,1:T(8,128)(2,1)}, bf16[512,64]{0,1:T(8,128)(2,1)S(1)}, u32[]{:S(2)}) copy-start(bf16[512,64]{0,1:T(8,128)(2,1)S(1)} %add_convert_fusion) | copy-start | bytes 196612
  92.4 10.8 %copy-start.11 = (s32[384]{0:T(512)S(1)}, s32[384]{0:T(512)}, u32[]{:S(2)}) copy-start(s32[384]{0:T(512)} %param.27) | copy-start | bytes 4612
  94.3 8.8 %all-to-all-start.2 = ((s32[8,2,2]{1,2,0:T(2,128)}), s32[8,2,2]{1,2,0:T(2,128)S(1)}, u32[]{:S(2)}, u32[]{:S(2)}) async-start(s32[8,2,2]{1,2,0:T(2,128)} %copy.97), calls=%async_computation.2 | async-start | bytes 16384 | tf_op jit(solution)/shard_map/all_to_all | solution.py:145
  103.1 40.8 %copy-start.10 = (f32[1024]{0:T(1024)S(1)}, f32[1024]{0:T(1024)}, u32[]{:S(2)}) copy-start(f32[1024]{0:T(1024)} %param.29) | copy-start | bytes 12292
  140.7 3.4 %copy-start.2 = (bf16[16,2048,64]{1,2,0:T(8,128)(2,1)S(1)}, bf16[16,2048,64]{1,2,0:T(8,128)(2,1)}, u32[]{:S(2)}) copy-start(bf16[16,2048,64]{1,2,0:T(8,128)(2,1)} %all-gather.2.cloned.1.call-done) | copy-start | bytes 12582916
  144.9 5.1 %copy-start.14 = (bf16[1024,1024]{1,0:T(8,128)(2,1)S(1)}, bf16[1024,1024]{1,0:T(8,128)(2,1)}, u32[]{:S(2)}) copy-start(bf16[1024,1024]{1,0:T(8,128)(2,1)} %param.32) | copy-start | bytes 6291460
  150.0 5.1 %copy-start.5 = (bf16[48,8,8,128]{3,2,1,0:T(8,128)(2,1)S(1)}, bf16[48,8,8,128]{3,2,1,0:T(8,128)(2,1)}, u32[]{:S(2)}) copy-start(bf16[48,8,8,128]{3,2,1,0:T(8,128)(2,1)} %fusion.30) | copy-start | bytes 2359300
  177.6 12.1 %copy-start.3 = (bf16[1024,1024]{1,0:T(8,128)(2,1)S(1)}, bf16[1024,1024]{1,0:T(8,128)(2,1)}, u32[]{:S(2)}) copy-start(bf16[1024,1024]{1,0:T(8,128)(2,1)} %param.33) | copy-start | bytes 6291460
  177.6 35.1 %copy-start.1 = (bf16[1024,1024]{1,0:T(8,128)(2,1)S(1)}, bf16[1024,1024]{1,0:T(8,128)(2,1)}, u32[]{:S(2)}) copy-start(bf16[1024,1024]{1,0:T(8,128)(2,1)} %param.31) | copy-start | bytes 6291460
  191.5 19.6 %all-to-all-start.3 = ((bf16[16,24,1024]{2,1,0:T(8,128)(2,1)}), bf16[16,24,1024]{2,1,0:T(8,128)(2,1)S(1)}, u32[]{:S(2)}, u32[]{:S(2)}) async-start(bf16[16,24,1024]{2,1,0:T(8,128)(2,1)} %bitcast.20), calls=%async_computation.3 | async-start | bytes 1572864 | tf_op jit(solution)/shard_map/all_to_all | solution.py:25
Sparse Core Ops, SparseCore 0:
  93.4 47.2 all-gather.1
